TPU v7x, 256 devices: a whole 4x4x8 slice. The times are simulated.
256 devices in a mesh: section: 16 (over z_lo, y), ctx: 4 (over x), tensor: 4 (over z_hi, core).
Axes of the slice: x: 4, y: 4, z: 8 (z_hi: 2, z_lo: 4; z = z_hi * 4 + z_lo), core: 2. Of those that a mesh axis runs over, the one named last changes fastest.
Arguments:
- arriving: bfloat16 [16, 1024, 4096], P('section', 'ctx', 'tensor')
- stored: bfloat16 [16, 1024, 4096], P('section', 'ctx', 'tensor')
- docs_forward: int32 [16, 1024], P('section', 'ctx'), may hold values from 0 to 3, never falling along the last dimension, each value on 1 to 512 neighbouring positions
- docs_backward: int32 [16, 1024], P('section', 'ctx'), may hold values from 0 to 3, never falling along the last dimension, each value on 1 to 512 neighbouring positions
- norm_gain: bfloat16 [16, 4096], P('section')
- query_weight: bfloat16 [16, 4096, 4096], P('section', 'ctx', 'tensor')
- key_weight: bfloat16 [16, 4096, 512], P('section', 'ctx', 'tensor')
- value_projection_weight: bfloat16 [16, 4096, 512], P('section', 'ctx', 'tensor'), may hold values from -0.09375 to 0.09375
- out_weight: bfloat16 [16, 4096, 4096], P('section', 'tensor', 'ctx'), may hold values from -0.375 to 0.375
Outputs:
- forward_output: bfloat16 [16, 1024, 4096], P('section', 'ctx', 'tensor')
- stashed: bfloat16 [16, 1024, 4096], P('section', 'ctx', 'tensor')
- rebuilt: bfloat16 [16, 1024, 4096], P('section', 'ctx', 'tensor')
Inputs may be any that keep to these rules, and one draw needn't show every extreme that they name: `docs_forward`: each row holds 4 packed documents: ids never fall, each document has 1 to 512 tokens, one exactly 512. `docs_backward`: each row holds 4 packed documents: ids never fall, each document has 1 to 512 tokens, one exactly 512.
All inputs are finite; a program needn't handle non-finite values.
Results may differ from a plain program's by a relative error of at most 0.0066.
Values may be sent and summed in bfloat16 or wider, within the bound.
No kernel may reach another device: no remote copies, remote signals or barrier semaphores. Data moves between devices by JAX's collectives and lax.ppermute only.
A program may use at most 128 MiB of HBM per device.

v0:
```python
import math
import jax
import jax.numpy as jnp
from jax import lax
from jax.sharding import PartitionSpec as P

HEAD = 128
QH = 32
KVH = 4
norm_epsilon = 1e-05
rope_base = 500000.0


def from_partner(block, axis, distance):
    count = lax.axis_size(axis)
    route = []
    for low in range(count):
        high = low | 1 << distance
        if high != low and high < count:
            route += [(low, high), (high, low)]
    return lax.ppermute(block, axis, route)


def normalize(inputs, gain_row):
    values = inputs.astype(jnp.float32)
    mean_square = jnp.mean(values * values, axis=-1, keepdims=True)
    return (values * lax.rsqrt(mean_square + norm_epsilon) * gain_row.astype(jnp.float32)).astype(
        jnp.bfloat16
    )


def rotary(values, positions, head_size):
    half_size = head_size // 2
    tokens = values.shape[0]
    shaped = values.reshape(tokens, -1, head_size)
    exponent = jnp.arange(half_size).astype(jnp.float32) * (2.0 / head_size)
    inverse = jnp.exp(-exponent * math.log(rope_base))
    angles = positions.astype(jnp.float32)[:, None] * inverse[None, :]
    cosine_lookup = jnp.cos(angles)[:, None, :]
    sine_table = jnp.sin(angles)[:, None, :]
    first_half = shaped[:, :, :half_size]
    second_half = shaped[:, :, half_size:]
    turned = jnp.concatenate(
        (
            first_half * cosine_lookup - second_half * sine_table,
            second_half * cosine_lookup + first_half * sine_table,
        ),
        axis=2,
    )
    return turned.reshape(tokens, -1)


def attend(queries, key_rows, value_rows, query_positions, key_positions, query_docs, key_docs):
    query_count = queries.shape[0]
    key_count = key_rows.shape[0]
    group_count = key_rows.shape[1] // HEAD
    group_size = QH // KVH
    grouped = queries.reshape(query_count, group_count, group_size, HEAD)
    key_heads = key_rows.reshape(key_count, group_count, HEAD)
    value_heads = value_rows.reshape(key_count, group_count, HEAD)
    permitted_mask = (key_positions[None, :] <= query_positions[:, None]) & (
        key_docs[None, :] == query_docs[:, None]
    )
    scores = jnp.einsum(
        "qkgh,skh->kgqs", grouped, key_heads, preferred_element_type=jnp.float32
    ) * (1.0 / math.sqrt(HEAD))
    masked = jnp.where(permitted_mask[None, None], scores, -jnp.inf)
    row_peak = jnp.max(masked, axis=3, keepdims=True)
    weights = jnp.exp(masked - row_peak)
    totals = jnp.sum(weights, axis=3, keepdims=True)
    probabilities = weights.astype(jnp.bfloat16)
    mixed_heads = jnp.einsum(
        "kgqs,skh->qkgh", probabilities, value_heads, preferred_element_type=jnp.float32
    )
    mixed_heads = mixed_heads / jnp.transpose(totals, (2, 0, 1, 3))
    return mixed_heads.reshape(query_count, -1).astype(jnp.bfloat16)


def body(
    arriving,
    stored,
    docs_forward,
    docs_backward,
    norm_gain,
    query_weight,
    key_weight,
    value_projection_weight,
    out_weight,
):
    tok_rows = arriving.shape[1]
    top_bit = lax.axis_size("section").bit_length() - 2
    stashed, fetched = from_partner((arriving, stored), "section", top_bit)
    inputs = jnp.concatenate((arriving[0], fetched[0]), axis=0)
    full_rows = lax.all_gather(inputs, "tensor", axis=1, tiled=True)
    normed = normalize(full_rows, norm_gain[0])
    key_width = key_weight.shape[2]
    query_full, key_full, value_full, out_full = (
        lax.all_gather(query_weight[0], "ctx", axis=0, tiled=True),
        lax.all_gather(key_weight[0], "ctx", axis=0, tiled=True),
        lax.all_gather(value_projection_weight[0], "ctx", axis=0, tiled=True),
        lax.all_gather(out_weight[0], "ctx", axis=1, tiled=True),
    )
    query_raw = jnp.dot(normed, query_full, preferred_element_type=jnp.float32)
    key_raw = jnp.dot(normed, key_full, preferred_element_type=jnp.float32)
    value_raw = jnp.dot(normed, value_full, preferred_element_type=jnp.float32)
    offset = lax.axis_index("ctx") * tok_rows
    local_pos = offset + jnp.arange(tok_rows, dtype=jnp.int32)
    both_pos = jnp.concatenate((local_pos, local_pos), axis=0)
    queries = rotary(query_raw, both_pos, HEAD).astype(jnp.bfloat16)
    key_rows = rotary(key_raw, both_pos, HEAD).astype(jnp.bfloat16)
    value_rows = value_raw.astype(jnp.bfloat16)
    docs_pair = jnp.stack((docs_forward[0], docs_backward[0]), axis=0)
    all_keys, all_values, all_docs = (
        lax.all_gather(key_rows.reshape(2, tok_rows, key_width), "ctx", axis=1, tiled=True),
        lax.all_gather(value_rows.reshape(2, tok_rows, key_width), "ctx", axis=1, tiled=True),
        lax.all_gather(docs_pair, "ctx", axis=1, tiled=True),
    )
    key_pos = jnp.arange(all_keys.shape[1], dtype=jnp.int32)
    mixed_parts = []
    for batch_index in range(2):
        mixed_parts.append(
            attend(
                queries[batch_index * tok_rows : (batch_index + 1) * tok_rows],
                all_keys[batch_index],
                all_values[batch_index],
                local_pos,
                key_pos,
                docs_pair[batch_index],
                all_docs[batch_index],
            )
        )
    mixed_heads = jnp.concatenate(mixed_parts, axis=0)
    head_terms = jnp.dot(mixed_heads, out_full, preferred_element_type=jnp.float32)
    head_total = lax.psum_scatter(head_terms, "tensor", scatter_dimension=1, tiled=True)
    result = (inputs.astype(jnp.float32) + head_total).astype(jnp.bfloat16)
    return (result[:tok_rows][None], stashed, result[tok_rows:][None])


def solution(mesh):
    return jax.shard_map(
        body,
        mesh=mesh,
        in_specs=(
            P("section", "ctx", "tensor"),
            P("section", "ctx", "tensor"),
            P("section", "ctx"),
            P("section", "ctx"),
            P("section", None),
            P("section", "ctx", "tensor"),
            P("section", "ctx", "tensor"),
            P("section", "ctx", "tensor"),
            P("section", "tensor", "ctx"),
        ),
        out_specs=(
            P("section", "ctx", "tensor"),
            P("section", "ctx", "tensor"),
            P("section", "ctx", "tensor"),
        ),
        check_vma=False,
    )
```

profile of v0, /device:TPU:1, one launch (start us, length us, event | category | flops | bytes accessed | tf_op | source)
XLA Modules:
  0.0 493.1 jit_solution(5165739500692440030)
XLA Ops:
  7.2 0.0 all-gather.10.cloned.1.call-start
  7.2 3.9 collective-permute-start
  11.1 22.4 %collective-permute-done = bf16[1,256,1024]{2,1,0:T(8,128)(2,1)S(1)} collective-permute-done((bf16[1,256,1024]{2,1,0:T(8,128)(2,1)}, bf16[1,256,1024]{2,1,0:T(8,128)(2,1)S(1)}, u32[]{:S(2)}, u32[]{:S(2)}) %collective-permute-start) | collective-permute-done | bytes 524320 | tf_op jit(solution)/shard_map/ppermute | solution.py:21
  33.6 2.1 pad_maximum_fusion
  35.7 0.0 all-gather.14.cloned.1.call-start
  35.7 0.7 all-gather.14.cloned.1.call-update
  36.4 0.0 all-gather.12.cloned.1.call-start
  36.5 0.7 all-gather.12.cloned.1.call-update
  37.1 0.0 all-gather.16.cloned.1.call-start
  37.2 0.5 all-gather.16.cloned.1.call-update
  37.7 0.0 all-gather.18.cloned.1.call-start
  37.8 0.5 all-gather.18.cloned.1.call-update
  38.3 0.0 reduce-scatter.2.cloned.1.call-start
  38.4 0.7 mul.176
  39.1 0.7 pad_add_fusion
  39.8 9.1 %all_gather.27 = s32[2,1024]{1,0:T(2,128)S(1)} all-gather(s32[2,256]{1,0:T(2,128)S(1)} %pad_add_fusion), channel_id=1, replica_groups=mesh['section'=16,'ctx'=4,'tensor'=4] {'ctx'}, dimensions={1}, use_global_device_ids=true | all-gather | bytes 10240 | tf_op jit(solution)/shard_map/all_gather | solution.py:116
  49.0 1.0 multiply_cosine_fusion
  50.0 0.7 fusion.36
  50.7 55.7 %all-gather.10.cloned.1.call-done = bf16[512,4096]{1,0:T(8,128)(2,1)} async-done(((bf16[512,1024]{1,0:T(8,128)(2,1)}), bf16[512,4096]{1,0:T(8,128)(2,1)}) %all-gather.10.cloned.1.call-update) | async-done | bytes 4194320 | tf_op jit(solution)/shard_map/all_gather | solution.py:94
  106.3 3.1 fusion
  109.4 20.0 %all-gather.14.cloned.1.call-done = bf16[1,4096,128]{2,1,0:T(8,128)(2,1)} async-done(((bf16[1,1024,128]{2,1,0:T(8,128)(2,1)}), bf16[1,4096,128]{2,1,0:T(8,128)(2,1)}) %all-gather.14.cloned.1.call-update) | async-done | bytes 1048592 | tf_op jit(solution)/shard_map/all_gather | solution.py:99
  129.5 4.1 convolution_bitcast_fusion
  133.6 0.6 fusion.51
  134.2 0.1 copy.20
  134.3 23.9 %all-gather.12.cloned.1.call-done = bf16[1,4096,128]{2,1,0:T(8,128)(2,1)} async-done(((bf16[1,1024,128]{2,1,0:T(8,128)(2,1)}), bf16[1,4096,128]{2,1,0:T(8,128)(2,1)}) %all-gather.12.cloned.1.call-update) | async-done | bytes 1048592 | tf_op jit(solution)/shard_map/all_gather | solution.py:100
  158.2 3.8 convolution_convert_fusion
  162.0 0.1 copy.12
  162.1 11.3 %all_gather.29 = bf16[2,1024,128]{2,1,0:T(8,128)(2,1)S(1)} all-gather(bf16[2,256,128]{2,1,0:T(8,128)(2,1)S(1)} %bitcast.131), channel_id=1, replica_groups=mesh['section'=16,'ctx'=4,'tensor'=4] {'ctx'}, dimensions={1}, use_global_device_ids=true | all-gather | bytes 655360 | tf_op jit(solution)/shard_map/all_gather | solution.py:114
  173.4 12.5 %all_gather.26 = bf16[2,1024,128]{1,2,0:T(8,128)(2,1)S(1)} all-gather(bf16[2,256,128]{1,2,0:T(8,128)(2,1)S(1)} %copy.12), channel_id=1, replica_groups=mesh['section'=16,'ctx'=4,'tensor'=4] {'ctx'}, dimensions={1}, use_global_device_ids=true | all-gather | bytes 655360 | tf_op jit(solution)/shard_map/all_gather | solution.py:115
  186.0 64.5 %all-gather.16.cloned.1.call-done = bf16[1,4096,1024]{2,1,0:T(8,128)(2,1)} async-done(((bf16[1,1024,1024]{2,1,0:T(8,128)(2,1)}), bf16[1,4096,1024]{2,1,0:T(8,128)(2,1)}) %all-gather.16.cloned.1.call-update) | async-done | bytes 8388624 | tf_op jit(solution)/shard_map/all_gather | solution.py:98
  250.5 8.2 %fusion.21 = f32[64,8,8,128]{3,1,2,0:T(8,128)S(1)} fusion(bf16[1,4096,1024]{2,1,0:T(8,128)(2,1)} %all-gather.16.cloned.1.call-done, bf16[512,4096]{1,0:T(8,128)(2,1)} %all-gather.10.cloned.1.call-done, f32[4096]{0:T(1024)S(1)} %bitcast.137, f32[512]{0:T(512)S(1)} %add_rsqrt_fusion), kind=kOutput, calls=%fused_computation.28 | convolution fusion | flops 4303355904 | bytes 14698496 | tf_op jit(solution)/shard_map/dot_general | solution.py:103
  258.7 0.5 copy.23
  259.2 0.7 fusion.64
  259.9 0.8 subtract_convert_fusion
  260.7 1.6 fusion.11
  262.3 1.7 fusion.12
  264.0 3.7 fusion.7
  267.7 2.3 divide_convert_fusion.1
  270.0 2.2 divide_convert_fusion
  272.2 66.4 %all-gather.18.cloned.1.call-done = bf16[1,1024,4096]{2,1,0:T(8,128)(2,1)} async-done(((bf16[1,1024,1024]{2,1,0:T(8,128)(2,1)}), bf16[1,1024,4096]{2,1,0:T(8,128)(2,1)}) %all-gather.18.cloned.1.call-update) | async-done | bytes 8388624 | tf_op jit(solution)/shard_map/all_gather | solution.py:101
  338.6 10.2 %fusion.3 = f32[512,4096]{1,0:T(8,128)} fusion(bf16[1,1024,4096]{2,1,0:T(8,128)(2,1)} %all-gather.18.cloned.1.call-done, bf16[256,1024]{0,1:T(8,128)(2,1)S(1)} %bitcast.130, bf16[256,1024]{0,1:T(8,128)(2,1)S(1)} %bitcast.129), kind=kOutput, calls=%fused_computation.7 | convolution fusion | flops 4297064448 | bytes 17825792 | tf_op jit(solution)/shard_map/dot_general | solution.py:133
  348.9 1.0 copy-done
  349.9 2.3 collective-permute-start.1
  352.2 22.7 %collective-permute-done.1 = bf16[1,256,1024]{2,1,0:T(8,128)(2,1)S(1)} collective-permute-done((bf16[1,256,1024]{2,1,0:T(8,128)(2,1)S(1)}, bf16[1,256,1024]{2,1,0:T(8,128)(2,1)S(1)}, u32[]{:S(2)}, u32[]{:S(2)}) %collective-permute-start.1) | collective-permute-done | bytes 524320 | tf_op jit(solution)/shard_map/ppermute | solution.py:21
  374.9 107.6 %reduce-scatter.2.cloned.1.call-done = f32[512,1024]{1,0:T(8,128)} async-done(((f32[512,4096]{1,0:T(8,128)}), f32[512,1024]{1,0:T(8,128)}) %reduce-scatter.2.cloned.1.call-update) | async-done | bytes 2097168 | tf_op jit(solution)/shard_map/reduce_scatter | solution.py:134
  482.5 1.9 add_convert_fusion
  484.4 1.0 slice_bitcast_fusion
  485.5 0.8 copy.29
  (13 shorter events, 0.1 us)
Async XLA Ops:
  7.2 42.8 %copy-start.1 = (s32[1,256]{1,0:T(1,128)S(1)}, s32[1,256]{1,0:T(1,128)}, u32[]{:S(2)}) copy-start(s32[1,256]{1,0:T(1,128)} %param.11) | copy-start | bytes 3076
  7.2 42.8 %copy-start.2 = (s32[1,256]{1,0:T(1,128)S(1)}, s32[1,256]{1,0:T(1,128)}, u32[]{:S(2)}) copy-start(s32[1,256]{1,0:T(1,128)} %param.12) | copy-start | bytes 3076
  7.2 99.2 %all-gather.10.cloned.1.call-start = ((), (), s32[]{:S(2)}) async-start(), calls=%async_computation.1 | async-start | bytes 5242880 | tf_op jit(solution)/shard_map/all_gather | solution.py:94
  7.2 26.3 %collective-permute-start = (bf16[1,256,1024]{2,1,0:T(8,128)(2,1)}, bf16[1,256,1024]{2,1,0:T(8,128)(2,1)S(1)}, u32[]{:S(2)}, u32[]{:S(2)}) collective-permute-start(bf16[1,256,1024]{2,1,0:T(8,128)(2,1)} %param.10), channel_id=1, source_target_pairs={{0,128},{128,0},{16,144},{144,16},{32,160},{160,32},{48,176},{176,... | collective-permute-start | bytes 1572872 | tf_op jit(solution)/shard_map/ppermute | solution.py:21
  35.7 93.8 %all-gather.14.cloned.1.call-start = ((), (), s32[]{:S(2)}) async-start(), calls=%async_computation.4 | async-start | bytes 1310720 | tf_op jit(solution)/shard_map/all_gather | solution.py:99
  36.4 121.8 %all-gather.12.cloned.1.call-start = ((), (), s32[]{:S(2)}) async-start(), calls=%async_computation.3 | async-start | bytes 1310720 | tf_op jit(solution)/shard_map/all_gather | solution.py:100
  37.1 213.4 %all-gather.16.cloned.1.call-start = ((), (), s32[]{:S(2)}) async-start(), calls=%async_computation.5 | async-start | bytes 10485760 | tf_op jit(solution)/shard_map/all_gather | solution.py:98
  37.7 300.9 %all-gather.18.cloned.1.call-start = ((), (), s32[]{:S(2)}) async-start(), calls=%async_computation.6 | async-start | bytes 10485760 | tf_op jit(solution)/shard_map/all_gather | solution.py:101
  38.3 444.2 %reduce-scatter.2.cloned.1.call-start = ((), (), s32[]{:S(2)}) async-start(), calls=%async_computation.2 | async-start | bytes 10485760 | tf_op jit(solution)/shard_map/reduce_scatter | solution.py:134
  348.8 1.0 copy-start
  349.9 25.0 %collective-permute-start.1 = (bf16[1,256,1024]{2,1,0:T(8,128)(2,1)S(1)}, bf16[1,256,1024]{2,1,0:T(8,128)(2,1)S(1)}, u32[]{:S(2)}, u32[]{:S(2)}) collective-permute-start(bf16[1,256,1024]{2,1,0:T(8,128)(2,1)S(1)} %copy-done), channel_id=1, source_target_pairs={{0,128},{128,0},{16,144},{144,16},{32,160},{160,32},{48,176},{176,... | collective-permute-start | bytes 1572872 | tf_op jit(solution)/shard_map/ppermute | solution.py:21
Sparse Core Ops, SparseCore 0:
  35.8 70.5 all-gather.9
  108.1 21.2 all-gather.13
  131.3 26.8 all-gather.11
  159.8 90.6 all-gather.15
  252.2 86.4 all-gather.17
  349.0 133.4 reduce-scatter.1
where the time goes:
time: 493 us
  waiting for transfers between devices  386 us (78%)
  matrix products  34.1 us (7%)
  blocking collectives  33 us (7%)
  other arithmetic  15.3 us (3%)
  between operations  14.3 us (3%)
  starting transfers between devices  6.4 us (1%)
    reduce_scatter x1, waiting for transfers between devices, body(): lax.psum_scatter(head_terms, 'tensor', scatter_dimension=1, tiled=True)  108 us
    all_gather x1, waiting for transfers between devices, body(): lax.all_gather(out_weight[0], 'ctx', axis=1, tiled=True)  66.4 us
    all_gather x1, waiting for transfers between devices, body(): lax.all_gather(query_weight[0], 'ctx', axis=0, tiled=True)  64.5 us
    all_gather x1, waiting for transfers between devices, body(): full_rows = lax.all_gather(inputs, 'tensor', axis=1, tiled=True)  55.7 us
    ppermute x2, waiting for transfers between devices, from_partner(): return lax.ppermute(block, axis, route)  45.1 us
    all_gather x1, waiting for transfers between devices, body(): lax.all_gather(value_projection_weight[0], 'ctx', axis=0, tiled=True)  23.9 us
    all_gather x1, waiting for transfers between devices, body(): lax.all_gather(key_weight[0], 'ctx', axis=0, tiled=True)  20 us
    all_gather x1, blocking collectives, body(): lax.all_gather(value_rows.reshape(2, tok_rows, key_width), 'ctx', axis=1,...  12.5 us
  transfers between devices with their start and end apart: 8, of which 8 were waited for; matrix products, arithmetic and copies ran while one was open for 7% of the time, Pallas kernels for 0%

commit v1 on v0

--- a/solution.py
+++ b/solution.py
@@ -1,3 +1,4 @@
+import functools
 import math
 import jax
 import jax.numpy as jnp
@@ -9,6 +10,15 @@
 KVH = 4
 norm_epsilon = 1e-05
 rope_base = 500000.0
+
+
+def counts_launch(arr, axis_name):
+    back = lax.all_to_all(jnp.stack([arr] * lax.axis_size(axis_name)), axis_name, 0, 0)
+    v_next = jnp.concatenate(back, axis=0)
+    return v_next
+
+
+reach_ticks = functools.partial(counts_launch, axis_name="ctx")
 
 
 def from_partner(block, axis, distance):
@@ -96,7 +106,7 @@
     key_width = key_weight.shape[2]
     query_full, key_full, value_full, out_full = (
         lax.all_gather(query_weight[0], "ctx", axis=0, tiled=True),
-        lax.all_gather(key_weight[0], "ctx", axis=0, tiled=True),
+        reach_ticks(key_weight[0]),
         lax.all_gather(value_projection_weight[0], "ctx", axis=0, tiled=True),
         lax.all_gather(out_weight[0], "ctx", axis=1, tiled=True),
     )

time: 493 us -> 465 us (0.943)
  waiting for transfers between devices: 386 us -> 344 us
  blocking collectives: 33 us -> 40.6 us
    all_gather x1 -> x0, waiting for transfers between devices: 20 us -> none  [body(): lax.all_gather(key_weight[0], 'ctx', axis=0, tiled=True)]
    all_gather x1, waiting for transfers between devices: 55.7 us -> 43.4 us  [body(): full_rows = lax.all_gather(inputs, 'tensor', axis=1, tiled=True)]
    all_gather x1, waiting for transfers between devices: 23.9 us -> 15.5 us  [body(): lax.all_gather(value_projection_weight[0], 'ctx', axis=0, tiled=True)]
    all_gather x1, blocking collectives: 9.1 us -> 16.7 us  [body(): lax.all_gather(docs_pair, 'ctx', axis=1, tiled=True)]
  transfers between devices with their start and end apart: 8 -> 8, of which waited for: 8 -> 7; matrix products, arithmetic and copies ran while one was open for 7% -> 8% of each run, Pallas kernels for 0% -> 0%
where the time goes in v1:
time: 465 us; the launch traced here: 464 us
  waiting for transfers between devices  344 us (74%)
  blocking collectives  40.6 us (9%)
  matrix products  33.8 us (7%)
  other arithmetic  14 us (3%)
  between operations  14 us (3%)
  starting transfers between devices  11 us (2%)
  local copies, waits for them, and re-layouts  6.32 us (1%)
    reduce_scatter x1, waiting for transfers between devices, body(): lax.psum_scatter(head_terms, 'tensor', scatter_dimension=1, tiled=True)  108 us
    all_gather x1, waiting for transfers between devices, body(): lax.all_gather(out_weight[0], 'ctx', axis=1, tiled=True)  66.3 us
    all_gather x1, waiting for transfers between devices, body(): lax.all_gather(query_weight[0], 'ctx', axis=0, tiled=True)  64.7 us
    ppermute x2, waiting for transfers between devices, from_partner(): return lax.ppermute(block, axis, route)  45.1 us
    all_gather x1, waiting for transfers between devices, body(): full_rows = lax.all_gather(inputs, 'tensor', axis=1, tiled=True)  43.4 us
    all_gather x1, blocking collectives, body(): lax.all_gather(docs_pair, 'ctx', axis=1, tiled=True)  16.7 us
    all_gather x1, waiting for transfers between devices, body(): lax.all_gather(value_projection_weight[0], 'ctx', axis=0, tiled=True)  15.5 us
    all_gather x1, blocking collectives, body(): lax.all_gather(value_rows.reshape(2, tok_rows, key_width), 'ctx', axis=1,...  12.5 us
  transfers between devices with their start and end apart: 8, of which 7 were waited for; matrix products, arithmetic and copies ran while one was open for 8% of the time, Pallas kernels for 0%

profile of v1, /device:TPU:1, one launch (start us, length us, event | category | flops | bytes accessed | tf_op | source)
XLA Modules:
  0.0 464.1 jit_solution(10069271927594653530)
XLA Ops:
  7.2 0.0 copy-start.1
  7.2 0.0 all-gather.8.cloned.1.call-start
  7.2 3.9 collective-permute-start
  11.1 22.4 %collective-permute-done = bf16[1,256,1024]{2,1,0:T(8,128)(2,1)S(1)} collective-permute-done((bf16[1,256,1024]{2,1,0:T(8,128)(2,1)}, bf16[1,256,1024]{2,1,0:T(8,128)(2,1)S(1)}, u32[]{:S(2)}, u32[]{:S(2)}) %collective-permute-start) | collective-permute-done | bytes 524320 | tf_op jit(solution)/shard_map/ppermute | solution.py:31
  33.6 2.1 pad_maximum_fusion
  35.7 0.0 all-gather.8.cloned.1.call-update
  35.7 0.0 all-gather.10.cloned.1.call-start
  35.7 0.7 all-gather.10.cloned.1.call-update
  36.5 0.0 all-gather.12.cloned.1.call-start
  36.5 0.7 all-gather.12.cloned.1.call-update
  37.2 0.0 all-gather.14.cloned.1.call-start
  37.2 0.5 all-gather.14.cloned.1.call-update
  37.8 2.1 stack.7
  39.9 4.7 %all-to-all-start = ((bf16[4,1024,128]{2,1,0:T(8,128)(2,1)}), bf16[4,1024,128]{2,1,0:T(8,128)(2,1)S(1)}, u32[]{:S(2)}, u32[]{:S(2)}) async-start(bf16[4,1024,128]{2,1,0:T(8,128)(2,1)} %stack.7), calls=%async_computation | async-start | bytes 2097152 | tf_op jit(solution)/shard_map/all_to_all | solution.py:16
  44.6 16.7 %all_gather.24 = s32[2,1024]{1,0:T(2,128)S(1)} all-gather(s32[2,256]{1,0:T(2,128)S(1)} %pad_add_fusion), channel_id=1, replica_groups=mesh['section'=16,'ctx'=4,'tensor'=4] {'ctx'}, dimensions={1}, use_global_device_ids=true | all-gather | bytes 10240 | tf_op jit(solution)/shard_map/all_gather | solution.py:126
  61.3 0.7 fusion.35
  62.0 1.0 multiply_cosine_fusion
  63.0 43.4 %all-gather.8.cloned.1.call-done = bf16[512,4096]{1,0:T(8,128)(2,1)} async-done(((bf16[512,1024]{1,0:T(8,128)(2,1)}), bf16[512,4096]{1,0:T(8,128)(2,1)}) %all-gather.8.cloned.1.call-update) | async-done | bytes 4194320 | tf_op jit(solution)/shard_map/all_gather | solution.py:104
  106.4 3.1 fusion
  109.5 0.0 all-to-all-done
  109.5 3.8 convolution_bitcast_fusion
  113.3 0.6 fusion.50
  113.9 0.1 copy.20
  114.0 15.5 %all-gather.10.cloned.1.call-done = bf16[1,4096,128]{2,1,0:T(8,128)(2,1)} async-done(((bf16[1,1024,128]{2,1,0:T(8,128)(2,1)}), bf16[1,4096,128]{2,1,0:T(8,128)(2,1)}) %all-gather.10.cloned.1.call-update) | async-done | bytes 1048592 | tf_op jit(solution)/shard_map/all_gather | solution.py:110
  129.5 3.8 convolution_convert_fusion
  133.3 0.1 copy.12
  133.4 11.3 %all_gather.25 = bf16[2,1024,128]{2,1,0:T(8,128)(2,1)S(1)} all-gather(bf16[2,256,128]{2,1,0:T(8,128)(2,1)S(1)} %bitcast.132), channel_id=1, replica_groups=mesh['section'=16,'ctx'=4,'tensor'=4] {'ctx'}, dimensions={1}, use_global_device_ids=true | all-gather | bytes 655360 | tf_op jit(solution)/shard_map/all_gather | solution.py:124
  144.8 12.5 %all_gather.23 = bf16[2,1024,128]{1,2,0:T(8,128)(2,1)S(1)} all-gather(bf16[2,256,128]{1,2,0:T(8,128)(2,1)S(1)} %copy.12), channel_id=1, replica_groups=mesh['section'=16,'ctx'=4,'tensor'=4] {'ctx'}, dimensions={1}, use_global_device_ids=true | all-gather | bytes 655360 | tf_op jit(solution)/shard_map/all_gather | solution.py:125
  157.3 64.7 %all-gather.12.cloned.1.call-done = bf16[1,4096,1024]{2,1,0:T(8,128)(2,1)} async-done(((bf16[1,1024,1024]{2,1,0:T(8,128)(2,1)}), bf16[1,4096,1024]{2,1,0:T(8,128)(2,1)}) %all-gather.12.cloned.1.call-update) | async-done | bytes 8388624 | tf_op jit(solution)/shard_map/all_gather | solution.py:108
  222.0 8.2 %fusion.21 = f32[64,8,8,128]{3,1,2,0:T(8,128)S(1)} fusion(bf16[1,4096,1024]{2,1,0:T(8,128)(2,1)} %all-gather.12.cloned.1.call-done, bf16[512,4096]{1,0:T(8,128)(2,1)} %all-gather.8.cloned.1.call-done, f32[4096]{0:T(1024)S(1)} %bitcast.139, f32[512]{0:T(512)S(1)} %add_rsqrt_fusion), kind=kOutput, calls=%fused_computation.28 | convolution fusion | flops 4303355904 | bytes 14698496 | tf_op jit(solution)/shard_map/dot_general | solution.py:113
  230.3 0.5 copy.23
  230.8 0.7 fusion.63
  231.4 0.8 subtract_convert_fusion
  232.2 1.6 fusion.11
  233.9 1.6 fusion.12
  235.5 3.7 fusion.7
  239.2 2.3 divide_convert_fusion.1
  241.5 2.2 divide_convert_fusion
  243.7 66.3 %all-gather.14.cloned.1.call-done = bf16[1,1024,4096]{2,1,0:T(8,128)(2,1)} async-done(((bf16[1,1024,1024]{2,1,0:T(8,128)(2,1)}), bf16[1,1024,4096]{2,1,0:T(8,128)(2,1)}) %all-gather.14.cloned.1.call-update) | async-done | bytes 8388624 | tf_op jit(solution)/shard_map/all_gather | solution.py:111
  310.0 10.2 %fusion.3 = f32[512,4096]{1,0:T(8,128)} fusion(bf16[1,1024,4096]{2,1,0:T(8,128)(2,1)} %all-gather.14.cloned.1.call-done, bf16[256,1024]{0,1:T(8,128)(2,1)S(1)} %bitcast.131, bf16[256,1024]{0,1:T(8,128)(2,1)S(1)} %bitcast.130), kind=kOutput, calls=%fused_computation.7 | convolution fusion | flops 4297064448 | bytes 17825792 | tf_op jit(solution)/shard_map/dot_general | solution.py:143
  320.2 0.0 reduce-scatter.2.cloned.1.call-update
  320.2 1.0 copy-done
  321.3 2.3 collective-permute-start.1
  323.5 22.7 %collective-permute-done.1 = bf16[1,256,1024]{2,1,0:T(8,128)(2,1)S(1)} collective-permute-done((bf16[1,256,1024]{2,1,0:T(8,128)(2,1)S(1)}, bf16[1,256,1024]{2,1,0:T(8,128)(2,1)S(1)}, u32[]{:S(2)}, u32[]{:S(2)}) %collective-permute-start.1) | collective-permute-done | bytes 524320 | tf_op jit(solution)/shard_map/ppermute | solution.py:31
  346.2 107.6 %reduce-scatter.2.cloned.1.call-done = f32[512,1024]{1,0:T(8,128)} async-done(((f32[512,4096]{1,0:T(8,128)}), f32[512,1024]{1,0:T(8,128)}) %reduce-scatter.2.cloned.1.call-update) | async-done | bytes 2097168 | tf_op jit(solution)/shard_map/reduce_scatter | solution.py:144
  453.8 1.9 add_convert_fusion
  455.8 1.0 slice_bitcast_fusion
  456.8 0.8 copy.29
  (15 shorter events, 0.1 us)
Async XLA Ops:
  7.2 37.4 %copy-start.1 = (bf16[1,4096]{1,0:T(2,128)(2,1)S(1)}, bf16[1,4096]{1,0:T(2,128)(2,1)}, u32[]{:S(2)}) copy-start(bf16[1,4096]{1,0:T(2,128)(2,1)} %param.13) | copy-start | bytes 24580
  7.2 37.4 %copy-start.2 = (s32[1,256]{1,0:T(1,128)S(1)}, s32[1,256]{1,0:T(1,128)}, u32[]{:S(2)}) copy-start(s32[1,256]{1,0:T(1,128)} %param.11) | copy-start | bytes 3076
  7.2 37.4 %copy-start.3 = (s32[1,256]{1,0:T(1,128)S(1)}, s32[1,256]{1,0:T(1,128)}, u32[]{:S(2)}) copy-start(s32[1,256]{1,0:T(1,128)} %param.12) | copy-start | bytes 3076
  7.2 99.2 %all-gather.8.cloned.1.call-start = ((), (), s32[]{:S(2)}) async-start(), calls=%async_computation.2 | async-start | bytes 5242880 | tf_op jit(solution)/shard_map/all_gather | solution.py:104
  7.2 26.3 %collective-permute-start = (bf16[1,256,1024]{2,1,0:T(8,128)(2,1)}, bf16[1,256,1024]{2,1,0:T(8,128)(2,1)S(1)}, u32[]{:S(2)}, u32[]{:S(2)}) collective-permute-start(bf16[1,256,1024]{2,1,0:T(8,128)(2,1)} %param.10), channel_id=1, source_target_pairs={{0,128},{128,0},{16,144},{144,16},{32,160},{160,32},{48,176},{176,... | collective-permute-start | bytes 1572872 | tf_op jit(solution)/shard_map/ppermute | solution.py:31
  35.7 93.8 %all-gather.10.cloned.1.call-start = ((), (), s32[]{:S(2)}) async-start(), calls=%async_computation.4 | async-start | bytes 1310720 | tf_op jit(solution)/shard_map/all_gather | solution.py:110
  36.5 185.6 %all-gather.12.cloned.1.call-start = ((), (), s32[]{:S(2)}) async-start(), calls=%async_computation.5 | async-start | bytes 10485760 | tf_op jit(solution)/shard_map/all_gather | solution.py:108
  37.2 272.8 %all-gather.14.cloned.1.call-start = ((), (), s32[]{:S(2)}) async-start(), calls=%async_computation.6 | async-start | bytes 10485760 | tf_op jit(solution)/shard_map/all_gather | solution.py:111
  39.9 69.6 %all-to-all-start = ((bf16[4,1024,128]{2,1,0:T(8,128)(2,1)}), bf16[4,1024,128]{2,1,0:T(8,128)(2,1)S(1)}, u32[]{:S(2)}, u32[]{:S(2)}) async-start(bf16[4,1024,128]{2,1,0:T(8,128)(2,1)} %stack.7), calls=%async_computation | async-start | bytes 2097152 | tf_op jit(solution)/shard_map/all_to_all | solution.py:16
  44.6 409.3 %reduce-scatter.2.cloned.1.call-start = ((), (), s32[]{:S(2)}) async-start(), calls=%async_computation.3 | async-start | bytes 10485760 | tf_op jit(solution)/shard_map/reduce_scatter | solution.py:144
  320.2 1.0 copy-start
  321.3 25.0 %collective-permute-start.1 = (bf16[1,256,1024]{2,1,0:T(8,128)(2,1)S(1)}, bf16[1,256,1024]{2,1,0:T(8,128)(2,1)S(1)}, u32[]{:S(2)}, u32[]{:S(2)}) collective-permute-start(bf16[1,256,1024]{2,1,0:T(8,128)(2,1)S(1)} %copy-done), channel_id=1, source_target_pairs={{0,128},{128,0},{16,144},{144,16},{32,160},{160,32},{48,176},{176,... | collective-permute-start | bytes 1572872 | tf_op jit(solution)/shard_map/ppermute | solution.py:31
Sparse Core Ops, SparseCore 0:
  35.8 70.5 all-gather.7
  108.2 21.2 all-gather.9
  131.3 90.6 all-gather.11
  223.7 86.2 all-gather.13
  320.4 133.4 reduce-scatter.1
